TPU v7x, 32 devices: a whole 2x2x4 slice. The times are simulated.
32 devices in a mesh: row: 4 (over z), col: 4 (over y, x), layer: 2 (over core).
Axes of the slice: x: 2, y: 2, z: 4, core: 2. Of those that a mesh axis runs over, the one named last changes fastest.
Arguments:
- ratings: bfloat16 [8192, 4096], P('row', ('col', 'layer')), may hold values from -6 to 6
- tile_mask: int32 [64, 32], P('row', ('col', 'layer')), may hold values 0 or 1
- tile_counts: int32 [64, 32], P('row', ('col', 'layer')), may hold values from 1 to 16384
- user_factor: float32 [256, 8192], P(('col', 'layer'), 'row'), may hold values from -1.5 to 1.5
- item_factor: float32 [256, 4096], P('row', ('col', 'layer')), may hold values from -1.5 to 1.5
Outputs:
- new_user: float32 [256, 8192], P(('col', 'layer'), 'row')
- new_item: float32 [256, 4096], P('row', ('col', 'layer'))
- loss_value: float32 [], replicated
- grad_norm: float32 [], replicated
All inputs are finite; a program needn't handle non-finite values. No bound on the sum of `tile_mask` on one device may be relied on, other than what follows from the above.
Results may differ from a plain program's by a relative error of at most 0.0049.
Values may be sent and summed in bfloat16 or wider, within the bound.
A program may use at most 64 MiB of HBM per device.

v0:
```python
import jax
import jax.numpy as jnp
from jax import lax
from jax.sharding import PartitionSpec as P

TILE = 128


epsilon = 1e-12
trust_ratio = 0.2


def tile_weights(mask_rows, count_rows):
    side = TILE
    position = lax.broadcasted_iota(jnp.int32, (side, side), 0) * side + lax.broadcasted_iota(
        jnp.int32, (side, side), 1
    )
    observed = (mask_rows[:, None, :, None] == 1) & (
        position[None, :, None, :] < count_rows[:, None, :, None]
    )
    return observed.astype(jnp.float32).reshape(
        mask_rows.shape[0] * side, mask_rows.shape[1] * side
    )


def body(ratings, tile_mask, tile_counts, user_factor, item_factor):
    user_low = user_factor.astype(jnp.bfloat16)
    item_low = item_factor.astype(jnp.bfloat16)
    user_rows = lax.all_gather(user_low, ("col", "layer"), axis=0, tiled=True)
    item_cols = lax.all_gather(item_low, "row", axis=0, tiled=True)
    count_local = jnp.sum(tile_mask * tile_counts).astype(jnp.float32)
    factor_local = jnp.sum(user_factor * user_factor) + jnp.sum(item_factor * item_factor)
    predicted = lax.dot_general(
        user_rows, item_cols, (((0,), (0,)), ((), ())), preferred_element_type=jnp.float32
    )
    residual = tile_weights(tile_mask, tile_counts) * (predicted - ratings.astype(jnp.float32))
    scaled = residual.astype(jnp.bfloat16)
    error_local = jnp.sum(residual * residual)
    count_sum, factor_sum, error_sum = lax.psum(
        (count_local, factor_local, error_local), ("row", "col", "layer")
    )
    factor_part = user_rows
    raw_item = lax.psum_scatter(
        jnp.dot(factor_part, scaled, preferred_element_type=jnp.float32).astype(jnp.bfloat16),
        "row",
        scatter_dimension=0,
        tiled=True,
    ).astype(jnp.float32)
    factor_part = item_cols
    raw_user = lax.psum_scatter(
        lax.dot_general(
            factor_part, scaled, (((1,), (1,)), ((), ())), preferred_element_type=jnp.float32
        ).astype(jnp.bfloat16),
        ("col", "layer"),
        scatter_dimension=0,
        tiled=True,
    ).astype(jnp.float32)
    gradient_local = jnp.sum(raw_user * raw_user) + jnp.sum(raw_item * raw_item)
    gradient_sum = lax.psum(gradient_local, ("row", "col", "layer"))
    observed_total = jnp.maximum(count_sum, jnp.float32(1.0))
    loss_value = error_sum / observed_total
    grad_norm = 2.0 / observed_total * jnp.sqrt(gradient_sum + epsilon)
    factor_norm = jnp.sqrt(factor_sum + epsilon)
    rate = trust_ratio * factor_norm / grad_norm
    step_size = rate * (2.0 / observed_total)
    new_user = user_factor - step_size * raw_user
    new_item = item_factor - step_size * raw_item
    return (new_user, new_item, loss_value, grad_norm)


def solution(mesh):
    return jax.shard_map(
        body,
        mesh=mesh,
        in_specs=(
            P("row", ("col", "layer")),
            P("row", ("col", "layer")),
            P("row", ("col", "layer")),
            P(("col", "layer"), "row"),
            P("row", ("col", "layer")),
        ),
        out_specs=(P(("col", "layer"), "row"), P("row", ("col", "layer")), P(), P()),
        check_vma=False,
    )
```

profile of v0, /device:TPU:0, one launch (start us, length us, event | category | flops | bytes accessed | tf_op | source)
XLA Modules:
  0.0 156.7 jit_solution(3589904584623122861)
XLA Ops:
  7.2 2.3 %multiply_reduce_fusion.1 = (f32[]{:T(128)}, bf16[32,2048]{1,0:T(8,128)(2,1)}) fusion(f32[32,2048]{1,0:T(8,128)} %param.8), kind=kLoop, calls=%fused_computation.17 | loop fusion | flops 196607 | bytes 393220 | tf_op jit(solution)/shard_map/reduce_sum | solution.py:32
  9.6 0.8 copy.16
  10.4 0.7 broadcast_compare_fusion
  11.2 1.6 %multiply_reduce_fusion.2 = (f32[]{:T(128)}, bf16[64,512]{1,0:T(8,128)(2,1)S(1)}) fusion(f32[64,512]{1,0:T(8,128)} %param.9), kind=kLoop, calls=%fused_computation.18 | loop fusion | flops 98303 | bytes 196612 | tf_op jit(solution)/shard_map/reduce_sum | solution.py:32
  12.8 15.6 %all_gather.7 = bf16[256,512]{1,0:T(8,128)(2,1)S(1)} all-gather(bf16[64,512]{1,0:T(8,128)(2,1)S(1)} %get-tuple-element.19), channel_id=1, replica_groups=mesh['row'=4,'col'=4,'layer'=2] {'row'}, dimensions={0}, use_global_device_ids=true | all-gather | bytes 327680 | tf_op jit(solution)/shard_map/all_gather | solution.py:30
  28.5 1.4 compare_and_fusion
  30.0 6.6 %all-gather.2.cloned.1.call-done = bf16[256,2048]{1,0:T(8,128)(2,1)} async-done(((bf16[32,2048]{1,0:T(8,128)(2,1)}), bf16[256,2048]{1,0:T(8,128)(2,1)}) %all-gather.2.cloned.1.call-update) | async-done | bytes 1048592 | tf_op jit(solution)/shard_map/all_gather | solution.py:29
  36.6 4.5 %multiply_reduce_fusion = (f32[]{:T(128)}, bf16[2048,512]{1,0:T(8,128)(2,1)S(1)}) fusion(bf16[2048,512]{1,0:T(8,128)(2,1)} %param.5, bf16[256,2048]{1,0:T(8,128)(2,1)} %all-gather.2.cloned.1.call-done, bf16[256,512]{1,0:T(8,128)(2,1)S(1)} %all_gather.7, pred[256,8,4,128]{3,2,1,0:T(4,128)(4,1)S(1)} %bitcast.16), kind=kOutput, calls=%fused_computation | convolution fusion | flops 543162368 | bytes 6553604 | tf_op jit(solution)/shard_map/dot_general | solution.py:33
  41.1 0.8 fusion.1
  41.8 0.8 copy.23
  42.7 0.7 fusion
  43.5 1.4 copy.21
  45.0 0.1 copy.18
  45.1 0.3 copy.17
  45.5 0.6 multiply_reduce_fusion.3
  48.0 14.8 %reduce-scatter.9.cloned.1.call-done = bf16[64,512]{1,0:T(8,128)(2,1)} async-done(((bf16[256,512]{1,0:T(8,128)(2,1)}), bf16[64,512]{1,0:T(8,128)(2,1)}) %reduce-scatter.9.cloned.1.call-update) | async-done | bytes 65552
  62.8 1.0 copy.24
  63.8 0.7 fusion.6
  64.5 35.8 %reduce-scatter.7.cloned.1.call-done = bf16[32,2048]{1,0:T(8,128)(2,1)} async-done(((bf16[256,2048]{1,0:T(8,128)(2,1)}), bf16[32,2048]{1,0:T(8,128)(2,1)}) %reduce-scatter.7.cloned.1.call-update) | async-done | bytes 131088
  100.3 1.2 copy.22
  101.4 0.9 fusion.2
  103.6 39.6 %all-reduce = (f32[]{:T(128)}, f32[]{:T(128)}, f32[]{:T(128)}, f32[]{:T(128)}) all-reduce(f32[]{:T(128)S(6)} %add.31, f32[]{:T(128)S(6)} %convert_element_type.35, f32[]{:T(128)S(6)} %add.34, f32[]{:T(128)} %get-tuple-element.20), channel_id=1, replica_groups=mesh['row'=4,'col'=4,'layer'=2] {'row','col','layer'}, use_global_device_ids=true, to_apply=%region_2.0 | all-reduce | flops 4 | bytes 32 | tf_op jit(solution)/shard_map/psum | solution.py:39
  145.3 0.8 copy.20
  146.2 1.0 copy.19
  (21 shorter events, 0.5 us)
Async XLA Ops:
  7.2 29.4 %all-gather.2.cloned.1.call-start = ((), (), s32[]{:S(2)}) async-start(), calls=%async_computation.2 | async-start | bytes 1179648 | tf_op jit(solution)/shard_map/all_gather | solution.py:29
  9.6 53.3 %reduce-scatter.9.cloned.1.call-start = ((), (), s32[]{:S(2)}) async-start(), calls=%async_computation.4 | async-start | bytes 327680
  36.6 4.5 %copy-start.4 = (bf16[256,2048]{1,0:T(8,128)(2,1)S(1)}, bf16[256,2048]{1,0:T(8,128)(2,1)}, u32[]{:S(2)}) copy-start(bf16[256,2048]{1,0:T(8,128)(2,1)} %all-gather.2.cloned.1.call-done) | copy-start | bytes 3145732
  42.7 57.6 %reduce-scatter.7.cloned.1.call-start = ((), (), s32[]{:S(2)}) async-start(), calls=%async_computation.3 | async-start | bytes 1179648
  43.5 1.5 copy-start.1
  43.5 1.6 %copy-start = (f32[32,2048]{1,0:T(8,128)S(1)}, f32[32,2048]{1,0:T(8,128)}, u32[]{:S(2)}) copy-start(f32[32,2048]{1,0:T(8,128)} %param.8) | copy-start | bytes 786436
  43.5 2.0 %copy-start.2 = (s32[16,4]{0,1:T(4,128)S(1)}, s32[16,4]{0,1:T(4,128)}, u32[]{:S(2)}) copy-start(s32[16,4]{0,1:T(4,128)} %param.7) | copy-start | bytes 772
  43.5 2.0 %copy-start.3 = (s32[16,4]{0,1:T(4,128)S(1)}, s32[16,4]{0,1:T(4,128)}, u32[]{:S(2)}) copy-start(s32[16,4]{0,1:T(4,128)} %param.6) | copy-start | bytes 772
Sparse Core Ops, SparseCore 0:
  10.4 26.0 all-gather.1
  42.8 19.9 reduce-scatter.8
  66.0 34.2 reduce-scatter.6
where the time goes:
time: 157 us
  waiting for transfers between devices  57.3 us (36%)
  blocking collectives  55.2 us (35%)
  between operations  22.1 us (14%)
  other arithmetic  8.47 us (5%)
  local copies, waits for them, and re-layouts  7.54 us (5%)
  matrix products  5.99 us (4%)
    unnamed x5, waiting for transfers between devices  50.7 us
    psum x1, blocking collectives, body(): lax.psum((count_local, factor_local, error_local), ('row', 'col', 'layer'))  39.6 us
    all_gather x1, blocking collectives, body(): item_cols = lax.all_gather(item_low, 'row', axis=0, tiled=True)  15.6 us
    unnamed x19, local copies, waits for them, and re-layouts  7.44 us
    all_gather x1, waiting for transfers between devices, body(): user_rows = lax.all_gather(user_low, ('col', 'layer'), axis=0, tiled=True)  6.59 us
    dot_general x1, matrix products, body(): lax.dot_general(user_rows, item_cols, (((0,), (0,)), ((), ())), preferred...  4.49 us
  transfers between devices with their start and end apart: 3, of which 3 were waited for; matrix products, arithmetic and copies ran while one was open for 6% of the time, Pallas kernels for 0%

commit v1 on v0

v1 whole, which is shorter than its diff:
```python
import math

import jax
import jax.numpy as jnp
from jax import lax
from jax.experimental import pallas as pl
from jax.experimental.pallas import tpu as pltpu
from jax.sharding import PartitionSpec as P

TILE = 128
epsilon = 1e-12
trust_ratio = 0.2
MESH = pl.DeviceIdType.MESH
CHUNKS = 4


def fold(value):
    flat = value.reshape(-1, value.shape[-1])
    rows = jnp.sum(flat.reshape(flat.shape[0] // 8, 8, flat.shape[1]), axis=0)
    total = rows[:, :TILE]
    for start in range(TILE, rows.shape[1], TILE):
        total = total + rows[:, start : start + TILE]
    return total


def make_step(nrow, ncol, nlay, rank, rows, cols):
    side = math.isqrt(ncol)
    ny = nx = side
    if side * side != ncol:
        ny, nx = 1, ncol
    ndev = nrow * ncol * nlay
    nplane = ncol * nlay
    urows, irows = rank // nplane, rank // nrow
    udt = jnp.bfloat16 if urows % 16 == 0 else jnp.float32
    idt = jnp.bfloat16 if irows % 16 == 0 else jnp.float32
    f32, bf16 = jnp.float32, jnp.bfloat16
    nch = CHUNKS
    width = rows // nch
    half = width // 2

    dxs, dys = range(1, nx), range(1, ny)
    dls, dzs = range(1, nlay), range(1, nrow)
    n_own = len(dxs) + len(dys) + len(dls)
    n_x, n_y = len(dxs), len(dys)
    per_chunk = (
        n_own
        + 2 * n_x * n_y
        + len(dls) * (n_x + n_y + 2 * n_x * n_y)
        + len(dls)
        + 2 * (n_x + n_y)
    )
    n_sems = nch * per_chunk + 2 * len(dzs)

    def kernel(
        mask, counts, ratings, user, item, raw_user, raw_item, stats,
        rat, uf, itf, U, I, pred, scaled, acc, PU, send0, recv0, S,
        send_a, recv_a, send_b, recv_b, SA, SB,
        send_a2, recv_a2, send_b2, recv_b2, out_u, out_i,
        send_i, recv_i, mine, G, rat_sem, in_sem, out_sem, ssem, rsem, gsend, grecv,
    ):
        z, c, l = lax.axis_index("row"), lax.axis_index("col"), lax.axis_index("layer")
        y, x = c // nx, c % nx

        def at(z_, y_, x_, l_):
            return (z_, y_ * nx + x_, l_)

        def xp(dx):
            return at(z, y, (x + dx) % nx, l)

        def yp(dy):
            return at(z, (y + dy) % ny, x, l)

        def lp(dl):
            return at(z, y, x, (l + dl) % nlay)

        def zp(dz):
            return at((z + dz) % nrow, y, x, l)

        def rank_of(y_, x_, l_):
            return (y_ * nx + x_) * nlay + l_

        load_u = pltpu.make_async_copy(user, uf, in_sem.at[0])
        load_i = pltpu.make_async_copy(item, itf, in_sem.at[1])
        load_u.start()
        load_i.start()
        loads = []
        for j in range(nch):
            part = pl.ds(j * width, width)
            load = pltpu.make_async_copy(ratings.at[part], rat.at[part], rat_sem.at[j])
            load.start()
            loads.append(load)

        barrier = pltpu.get_barrier_semaphore()
        peers = (
            [lp(d) for d in dls] + [xp(d) for d in dxs] + [yp(d) for d in dys] + [zp(d) for d in dzs]
        )
        for peer in peers:
            pl.semaphore_signal(barrier, inc=1, device_id=peer, device_id_type=MESH)

        me = rank_of(y, x, l)
        load_i.wait()
        I[z] = itf[...].astype(bf16).astype(idt)
        load_u.wait()
        U[me] = uf[...].astype(bf16).astype(udt)
        pl.semaphore_wait(barrier, len(peers))

        used = [0]
        pending = []

        def send(src, dst, peer):
            n = used[0]
            used[0] += 1
            copy = pltpu.make_async_remote_copy(
                src_ref=src, dst_ref=dst, send_sem=ssem.at[n], recv_sem=rsem.at[n],
                device_id=peer, device_id_type=MESH,
            )
            copy.start()
            pending.append(copy)
            return copy

        gathers_i = [send(I.at[z], I.at[z], zp(d)) for d in dzs]

        got_x, got_y, got_a, got_b, got_l = {}, {}, {}, {}, {}

        def block(j, y_, x_, l_, lo, size):
            return U.at[rank_of(y_, x_, l_), :, pl.ds(j * width + lo, size)]

        def own(j):
            b = block(j, y, x, l, 0, width)
            got_x[j] = [send(b, b, xp(d)) for d in dxs]
            got_y[j] = [send(b, b, yp(d)) for d in dys]
            got_l[j] = [send(b, b, lp(d)) for d in dls]

        def relay(j):
            got_a[j], got_b[j] = [], []
            for dx, copy in zip(dxs, got_x[j]):
                copy.wait_recv()
                sx = (x + nx - dx) % nx
                b = block(j, y, sx, l, 0, half)
                got_a[j] += [send(b, b, yp(d)) for d in dys]
            for dy, copy in zip(dys, got_y[j]):
                copy.wait_recv()
                sy = (y + ny - dy) % ny
                b = block(j, sy, x, l, half, half)
                got_b[j] += [send(b, b, xp(d)) for d in dxs]
            for dx in dxs:
                b = block(j, y, (x + nx - dx) % nx, l, 0, width)
                got_l[j] += [send(b, b, lp(d)) for d in dls]
            for dy in dys:
                b = block(j, (y + ny - dy) % ny, x, l, 0, width)
                got_l[j] += [send(b, b, lp(d)) for d in dls]

        def corner(j):
            n = 0
            for dx in dxs:
                for dy in dys:
                    got_a[j][n].wait_recv()
                    n += 1
                    b = block(j, (y + ny - dy) % ny, (x + nx - dx) % nx, l, 0, half)
                    got_l[j] += [send(b, b, lp(d)) for d in dls]
            n = 0
            for dy in dys:
                for dx in dxs:
                    got_b[j][n].wait_recv()
                    n += 1
                    b = block(j, (y + ny - dy) % ny, (x + nx - dx) % nx, l, half, half)
                    got_l[j] += [send(b, b, lp(d)) for d in dls]

        position = lax.broadcasted_iota(jnp.int32, (TILE, TILE), 0) * TILE + lax.broadcasted_iota(
            jnp.int32, (TILE, TILE), 1
        )
        got_0 = {}

        def compute(j, error):
            for copy in got_l[j]:
                copy.wait_recv()
            if j == 0:
                for copy in gathers_i:
                    copy.wait_recv()
            loads[j].wait()
            items = I[...].reshape(rank, cols).astype(bf16)
            users = U[:, :, j * width : (j + 1) * width].reshape(rank, width).astype(bf16)
            pred[...] = lax.dot_general(
                users, items, (((0,), (0,)), ((), ())), preferred_element_type=f32
            )

            def tiles(t, total):
                local = pl.ds(pl.multiple_of(t * TILE, TILE), TILE)
                whole = pl.ds(pl.multiple_of(j * width + t * TILE, TILE), TILE)
                row = j * (width // TILE) + t
                for k in range(cols // TILE):
                    lane = slice(k * TILE, (k + 1) * TILE)
                    limit = jnp.where(mask[row, k] == 1, counts[row, k], 0)
                    diff = pred[local, lane] - rat[whole, lane].astype(f32)
                    diff = jnp.where(position < limit, diff, 0.0)
                    scaled[local, lane] = diff.astype(bf16)
                    total = total + fold(diff * diff)
                return total

            error = lax.fori_loop(0, width // TILE, tiles, error)
            sc = scaled[...]
            PU[j] = lax.dot_general(
                items, sc, (((1,), (1,)), ((), ())), preferred_element_type=f32
            ).reshape(ncol, nlay, urows, width)
            got_0[j] = []
            for dl in dls:
                send0[j, dl - 1] = PU[j, :, (l + dl) % nlay].astype(udt)
                got_0[j].append(send(send0.at[j, dl - 1], recv0.at[j, dl - 1], lp(dl)))
            grad = jnp.dot(users, sc, preferred_element_type=f32).reshape(nrow, irows, cols)
            if j == 0:
                acc[...] = grad
            else:
                acc[...] += grad
            return error

        got_1a, got_1b, got_2a, got_2b = {}, {}, {}, {}

        def rs1(j):
            total = PU[j, :, l]
            for dl, copy in zip(dls, got_0[j]):
                copy.wait_recv()
                total = total + recv0[j, dl - 1].astype(f32)
            S[j] = total.reshape(ny, nx, urows, width)
            got_1a[j], got_1b[j] = [], []
            for dx in dxs:
                send_a[j, dx - 1] = S[j, :, (x + dx) % nx, :, :half].astype(udt)
                got_1a[j].append(send(send_a.at[j, dx - 1], recv_a.at[j, dx - 1], xp(dx)))
            for dy in dys:
                send_b[j, dy - 1] = S[j, (y + dy) % ny, :, :, half:].astype(udt)
                got_1b[j].append(send(send_b.at[j, dy - 1], recv_b.at[j, dy - 1], yp(dy)))

        def rs2(j):
            total = S[j, :, x, :, :half]
            for dx, copy in zip(dxs, got_1a[j]):
                copy.wait_recv()
                total = total + recv_a[j, dx - 1].astype(f32)
            SA[j] = total
            got_2a[j], got_2b[j] = [], []
            for dy in dys:
                send_a2[j, dy - 1] = SA[j, (y + dy) % ny].astype(udt)
                got_2a[j].append(send(send_a2.at[j, dy - 1], recv_a2.at[j, dy - 1], yp(dy)))
            total = S[j, y, :, :, half:]
            for dy, copy in zip(dys, got_1b[j]):
                copy.wait_recv()
                total = total + recv_b[j, dy - 1].astype(f32)
            SB[j] = total
            for dx in dxs:
                send_b2[j, dx - 1] = SB[j, (x + dx) % nx].astype(udt)
                got_2b[j].append(send(send_b2.at[j, dx - 1], recv_b2.at[j, dx - 1], xp(dx)))

        stores = []

        def rs3(j, grads):
            total = SA[j, y]
            for dy, copy in zip(dys, got_2a[j]):
                copy.wait_recv()
                total = total + recv_a2[j, dy - 1].astype(f32)
            out_u[:, j * width : j * width + half] = total
            grads = grads + fold(total * total)
            total = SB[j, x]
            for dx, copy in zip(dxs, got_2b[j]):
                copy.wait_recv()
                total = total + recv_b2[j, dx - 1].astype(f32)
            out_u[:, j * width + half : (j + 1) * width] = total
            grads = grads + fold(total * total)
            return grads

        error = jnp.zeros((8, TILE), f32)
        grads = jnp.zeros((8, TILE), f32)
        own(0)
        if nch > 1:
            own(1)
        relay(0)
        factor = fold(uf[...] * uf[...]) + fold(itf[...] * itf[...])
        got_z = []
        for j in range(nch + 3):
            if j + 2 < nch:
                own(j + 2)
            if j + 1 < nch:
                relay(j + 1)
            if j < nch:
                corner(j)
                error = compute(j, error)
            if j == nch - 1:
                for dz in dzs:
                    send_i[dz - 1] = acc[(z + dz) % nrow].astype(idt)
                    got_z.append(send(send_i.at[dz - 1], recv_i.at[dz - 1], zp(dz)))
            if 0 <= j - 1 < nch:
                rs1(j - 1)
            if 0 <= j - 2 < nch:
                rs2(j - 2)
            if 0 <= j - 3 < nch:
                grads = rs3(j - 3, grads)

        total = acc[z]
        for dz, copy in zip(dzs, got_z):
            copy.wait_recv()
            total = total + recv_i[dz - 1].astype(f32)
        out_i[...] = total
        grads = grads + fold(total * total)

        store_u = pltpu.make_async_copy(out_u, raw_user, out_sem.at[0])
        store_i = pltpu.make_async_copy(out_i, raw_item, out_sem.at[1])
        store_u.start()
        store_i.start()

        def count_of(t, total):
            for k in range(cols // TILE):
                total = total + jnp.where(mask[t, k] == 1, counts[t, k], 0)
            return total

        count = lax.fori_loop(0, rows // TILE, count_of, jnp.int32(0)).astype(f32)
        sub = lax.broadcasted_iota(jnp.int32, (8, TILE), 0)
        lane = lax.broadcasted_iota(jnp.int32, (8, TILE), 1)

        def spread(value):
            return jnp.broadcast_to(jnp.sum(value, axis=0, keepdims=True), (8, TILE))

        tile = jnp.where((sub == 3) & (lane == 0), count, 0.0)
        tile = jnp.where(sub == 0, spread(error), tile)
        tile = jnp.where(sub == 1, spread(factor), tile)
        tile = jnp.where(sub == 2, spread(grads), tile)
        mine[...] = tile
        flat = (z * ncol + c) * nlay + l
        G[flat] = tile

        def share(delta):
            to = (flat + delta) % ndev
            return pltpu.make_async_remote_copy(
                src_ref=mine, dst_ref=G.at[flat], send_sem=gsend, recv_sem=grecv,
                device_id=(to // nplane, (to // nlay) % ncol, to % nlay), device_id_type=MESH,
            )

        @pl.loop(1, ndev)
        def _(delta):
            share(delta).start()

        every = pl.ds(0, ndev - 1)
        pltpu.make_async_copy(G.at[every], G.at[every], grecv).wait()
        total = jnp.sum(G[...], axis=0)

        def pick(n):
            return jnp.sum(total[n : n + 1], axis=1, keepdims=True)

        error_sum, factor_sum, grad_sum = pick(0), pick(1), pick(2)
        observed = jnp.maximum(pick(3), 1.0)
        loss = error_sum / observed
        grad_norm = 2.0 / observed * jnp.sqrt(grad_sum + epsilon)
        rate = trust_ratio * jnp.sqrt(factor_sum + epsilon) / grad_norm
        step = rate * (2.0 / observed)
        result = jnp.where(sub == 0, loss, jnp.where(sub == 1, grad_norm, step))
        stats[...] = result
        for copy in pending:
            copy.wait_send()
        pltpu.make_async_copy(G.at[every], G.at[every], gsend).wait()
        store_u.wait()
        store_i.wait()

    vm = pltpu.VMEM
    dma = pltpu.SemaphoreType.DMA
    mx, my, ml, mz = max(nx - 1, 1), max(ny - 1, 1), max(nlay - 1, 1), max(nrow - 1, 1)
    smem = pl.BlockSpec(memory_space=pltpu.SMEM)
    hbm = pl.BlockSpec(memory_space=pl.ANY)
    return pl.pallas_call(
        kernel,
        out_shape=(
            jax.ShapeDtypeStruct((urows, rows), f32),
            jax.ShapeDtypeStruct((irows, cols), f32),
            jax.ShapeDtypeStruct((8, TILE), f32),
        ),
        in_specs=[smem, smem, hbm, hbm, hbm],
        out_specs=(hbm, hbm, pl.BlockSpec(memory_space=pltpu.VMEM)),
        scratch_shapes=[
            vm((rows, cols), bf16),
            vm((urows, rows), f32),
            vm((irows, cols), f32),
            vm((nplane, urows, rows), udt),
            vm((nrow, irows, cols), idt),
            vm((width, cols), f32),
            vm((width, cols), bf16),
            vm((nrow, irows, cols), f32),
            vm((nch, ncol, nlay, urows, width), f32),
            vm((nch, ml, ncol, urows, width), udt),
            vm((nch, ml, ncol, urows, width), udt),
            vm((nch, ny, nx, urows, width), f32),
            vm((nch, mx, ny, urows, half), udt),
            vm((nch, mx, ny, urows, half), udt),
            vm((nch, my, nx, urows, half), udt),
            vm((nch, my, nx, urows, half), udt),
            vm((nch, ny, urows, half), f32),
            vm((nch, nx, urows, half), f32),
            vm((nch, my, urows, half), udt),
            vm((nch, my, urows, half), udt),
            vm((nch, mx, urows, half), udt),
            vm((nch, mx, urows, half), udt),
            vm((urows, rows), f32),
            vm((irows, cols), f32),
            vm((mz, irows, cols), idt),
            vm((mz, irows, cols), idt),
            vm((8, TILE), f32),
            vm((ndev, 8, TILE), f32),
            dma((nch,)),
            dma((2,)),
            dma((2,)),
            dma((n_sems,)),
            dma((n_sems,)),
            dma(()),
            dma(()),
        ],
        compiler_params=pltpu.CompilerParams(collective_id=0, has_side_effects=True),
        name="completion_step",
    )


def solution(mesh):
    nrow, ncol, nlay = mesh.shape["row"], mesh.shape["col"], mesh.shape["layer"]

    def body(ratings, tile_mask, tile_counts, user_factor, item_factor):
        rows, cols = ratings.shape
        rank = user_factor.shape[0] * ncol * nlay
        step = make_step(nrow, ncol, nlay, rank, rows, cols)
        raw_user, raw_item, stats = step(tile_mask, tile_counts, ratings, user_factor, item_factor)
        step_size = stats[2, 0]
        new_user = user_factor - step_size * raw_user
        new_item = item_factor - step_size * raw_item
        return (new_user, new_item, stats[0, 0], stats[1, 0])

    return jax.shard_map(
        body,
        mesh=mesh,
        in_specs=(
            P("row", ("col", "layer")),
            P("row", ("col", "layer")),
            P("row", ("col", "layer")),
            P(("col", "layer"), "row"),
            P("row", ("col", "layer")),
        ),
        out_specs=(P(("col", "layer"), "row"), P("row", ("col", "layer")), P(), P()),
        check_vma=False,
    )
```

time: 157 us -> 46.2 us (0.29)
  waiting for transfers between devices: 57.3 us -> 0 us
  blocking collectives: 55.2 us -> 0 us
  Pallas kernels: 0 us -> 36.4 us
  between operations: 22.1 us -> 0.66 us
  matrix products: 5.99 us -> 0 us
  other arithmetic: 8.47 us -> 4.63 us
  local copies, waits for them, and re-layouts: 7.54 us -> 4.16 us
    unnamed x5 -> x0, waiting for transfers between devices: 50.7 us -> none
    psum x1 -> x0, blocking collectives: 39.6 us -> none  [body(): lax.psum((count_local, factor_local, error_local), ('row', 'col', 'layer'))]
    pallas_call x0 -> x1, Pallas kernels: none -> 36.4 us  [body(): step(tile_mask, tile_counts, ratings, user_factor, item_factor)]
    all_gather x1 -> x0, blocking collectives: 15.6 us -> none  [body(): item_cols = lax.all_gather(item_low, 'row', axis=0, tiled=True)]
    all_gather x1 -> x0, waiting for transfers between devices: 6.59 us -> none  [body(): user_rows = lax.all_gather(user_low, ('col', 'layer'), axis=0, tiled=True)]
    reduce_sum x5 -> x0, other arithmetic: 6.12 us -> none  [the longest x1 2.33 us: body(): jnp.sum(user_factor * user_factor) + jnp.sum(item_factor * item_factor)]
    dot_general x3 -> x0, matrix products: 5.99 us -> none  [the longest x1 4.49 us: body(): lax.dot_general(user_rows, item_cols, (((0,), (0,)), ((), ())), preferred...]
    unnamed x19 -> x6, local copies, waits for them, and re-layouts: 7.44 us -> 2.77 us
  transfers between devices with their start and end apart: 3 -> 0, of which waited for: 3 -> 0; matrix products, arithmetic and copies ran while one was open for 6% -> 0% of each run, Pallas kernels for 0% -> 0%
where the time goes in v1:
time: 46.2 us; the launch traced here: 45.8 us
  Pallas kernels  36.4 us (79%)
  other arithmetic  4.63 us (10%)
  local copies, waits for them, and re-layouts  4.16 us (9%)
  between operations  0.66 us (1%)
    pallas_call x1, Pallas kernels, body(): step(tile_mask, tile_counts, ratings, user_factor, item_factor)  36.4 us
    unnamed x6, local copies, waits for them, and re-layouts  2.77 us
    sub x1, other arithmetic, body(): new_user = user_factor - step_size * raw_user  2.37 us
    sub x1, other arithmetic, body(): new_item = item_factor - step_size * raw_item  2.26 us
    slice x1, local copies, waits for them, and re-layouts, body(): return (new_user, new_item, stats[0, 0], stats[1, 0])  1.39 us

profile of v1, /device:TPU:0, one launch (start us, length us, event | category | flops | bytes accessed | tf_op | source)
XLA Modules:
  0.0 45.8 jit_solution(2446504841618889062)
XLA Ops:
  0.6 0.0 copy-start.1
  0.6 0.0 copy-start
  0.7 1.4 %copy.9.mask = s32[16,4]{1,0:T(8,128)} copy(s32[16,4]{0,1:T(4,128)} %param.6) | data formatting | bytes 512 | tf_op args[1]
  2.1 1.4 %copy.10.counts = s32[16,4]{1,0:T(8,128)} copy(s32[16,4]{0,1:T(4,128)} %param.7) | data formatting | bytes 512 | tf_op args[2]
  3.4 36.4 %completion_step.1 = (f32[32,2048]{1,0:T(8,128)}, f32[64,512]{1,0:T(8,128)}, f32[8,128]{1,0:T(8,128)}) custom-call(s32[16,4]{1,0:T(8,128)} %copy.9.mask, s32[16,4]{1,0:T(8,128)} %copy.10.counts, bf16[2048,512]{1,0:T(8,128)(2,1)} %ratings.1, f32[32,2048]{1,0:T(8,128)} %user.1, f32[64,512]{1,0:T(8,128)} %item.1), custom_call_target="tpu_custom_call" | custom-call | tf_op jit(solution)/shard_map/completion_step/pallas_call | solution.py:422
  39.8 1.4 %fusion = (f32[1,1]{1,0:T(1,128)}, f32[1,1]{1,0:T(1,128)}, f32[1,1]{1,0:T(1,128)}) fusion(f32[8,128]{1,0:T(8,128)} %get-tuple-element.7), kind=kLoop, calls=%fused_computation.2 | loop fusion | bytes 24 | tf_op jit(solution)/shard_map/slice | solution.py:426
  41.2 0.0 copy-done.1
  41.2 2.3 %multiply_subtract_fusion.1 = f32[64,512]{1,0:T(8,128)} fusion(f32[64,512]{1,0:T(8,128)S(1)} %copy-done.1, f32[64,512]{1,0:T(8,128)} %get-tuple-element.9, f32[]{:T(128)} %bitcast), kind=kLoop, calls=%fused_computation.1 | loop fusion | flops 65536 | bytes 393220 | tf_op jit(solution)/shard_map/sub | solution.py:425
  43.4 0.0 copy-done
  43.4 2.4 %multiply_subtract_fusion = f32[32,2048]{1,0:T(8,128)} fusion(f32[32,2048]{1,0:T(8,128)S(1)} %copy-done, f32[32,2048]{1,0:T(8,128)} %get-tuple-element.8, f32[]{:T(128)} %bitcast), kind=kLoop, calls=%fused_computation | loop fusion | flops 131072 | bytes 786436 | tf_op jit(solution)/shard_map/sub | solution.py:424
Async XLA Ops:
  0.6 40.5 %copy-start.1 = (f32[64,512]{1,0:T(8,128)S(1)}, f32[64,512]{1,0:T(8,128)}, u32[]{:S(2)}) copy-start(f32[64,512]{1,0:T(8,128)} %item.1) | copy-start | bytes 393220
  0.6 42.8 %copy-start = (f32[32,2048]{1,0:T(8,128)S(1)}, f32[32,2048]{1,0:T(8,128)}, u32[]{:S(2)}) copy-start(f32[32,2048]{1,0:T(8,128)} %user.1) | copy-start | bytes 786436

commit v2 on v1

--- a/solution.py
+++ b/solution.py
@@ -11,7 +11,7 @@
 epsilon = 1e-12
 trust_ratio = 0.2
 MESH = pl.DeviceIdType.MESH
-CHUNKS = 4
+CHUNKS = 2
 
 
 def fold(value):
@@ -52,11 +52,11 @@
     n_sems = nch * per_chunk + 2 * len(dzs)
 
     def kernel(
-        mask, counts, ratings, user, item, raw_user, raw_item, stats,
+        mask, counts, ratings, user, item, out_u, out_i, stats,
         rat, uf, itf, U, I, pred, scaled, acc, PU, send0, recv0, S,
         send_a, recv_a, send_b, recv_b, SA, SB,
-        send_a2, recv_a2, send_b2, recv_b2, out_u, out_i,
-        send_i, recv_i, mine, G, rat_sem, in_sem, out_sem, ssem, rsem, gsend, grecv,
+        send_a2, recv_a2, send_b2, recv_b2,
+        send_i, recv_i, mine, G, rat_sem, in_sem, ssem, rsem, gsend, grecv,
     ):
         z, c, l = lax.axis_index("row"), lax.axis_index("col"), lax.axis_index("layer")
         y, x = c // nx, c % nx
@@ -190,7 +190,7 @@
                 row = j * (width // TILE) + t
                 for k in range(cols // TILE):
                     lane = slice(k * TILE, (k + 1) * TILE)
-                    limit = jnp.where(mask[row, k] == 1, counts[row, k], 0)
+                    limit = jnp.where(mask[k, row] == 1, counts[k, row], 0)
                     diff = pred[local, lane] - rat[whole, lane].astype(f32)
                     diff = jnp.where(position < limit, diff, 0.0)
                     scaled[local, lane] = diff.astype(bf16)
@@ -299,14 +299,9 @@
         out_i[...] = total
         grads = grads + fold(total * total)
 
-        store_u = pltpu.make_async_copy(out_u, raw_user, out_sem.at[0])
-        store_i = pltpu.make_async_copy(out_i, raw_item, out_sem.at[1])
-        store_u.start()
-        store_i.start()
-
         def count_of(t, total):
             for k in range(cols // TILE):
-                total = total + jnp.where(mask[t, k] == 1, counts[t, k], 0)
+                total = total + jnp.where(mask[k, t] == 1, counts[k, t], 0)
             return total
 
         count = lax.fori_loop(0, rows // TILE, count_of, jnp.int32(0)).astype(f32)
@@ -353,8 +348,6 @@
         for copy in pending:
             copy.wait_send()
         pltpu.make_async_copy(G.at[every], G.at[every], gsend).wait()
-        store_u.wait()
-        store_i.wait()
 
     vm = pltpu.VMEM
     dma = pltpu.SemaphoreType.DMA
@@ -369,7 +362,7 @@
             jax.ShapeDtypeStruct((8, TILE), f32),
         ),
         in_specs=[smem, smem, hbm, hbm, hbm],
-        out_specs=(hbm, hbm, pl.BlockSpec(memory_space=pltpu.VMEM)),
+        out_specs=(pl.BlockSpec(memory_space=pltpu.VMEM),) * 3,
         scratch_shapes=[
             vm((rows, cols), bf16),
             vm((urows, rows), f32),
@@ -393,14 +386,11 @@
             vm((nch, my, urows, half), udt),
             vm((nch, mx, urows, half), udt),
             vm((nch, mx, urows, half), udt),
-            vm((urows, rows), f32),
-            vm((irows, cols), f32),
             vm((mz, irows, cols), idt),
             vm((mz, irows, cols), idt),
             vm((8, TILE), f32),
             vm((ndev, 8, TILE), f32),
             dma((nch,)),
-            dma((2,)),
             dma((2,)),
             dma((n_sems,)),
             dma((n_sems,)),
@@ -412,6 +402,30 @@
     )
 
 
+def update(raw_user, raw_item, stats, user, item):
+    def kernel(gu, gi, st, fu, fi, new_u, new_i, loss, norm):
+        step = st[2:3, 0:1]
+        new_i[...] = fi[...] - step * gi[...]
+        new_u[...] = fu[...] - step * gu[...]
+        loss[...] = st[0:1, 0:1]
+        norm[...] = st[1:2, 0:1]
+
+    f32 = jnp.float32
+    whole = pl.BlockSpec(memory_space=pltpu.VMEM)
+    return pl.pallas_call(
+        kernel,
+        out_shape=(
+            jax.ShapeDtypeStruct(user.shape, f32),
+            jax.ShapeDtypeStruct(item.shape, f32),
+            jax.ShapeDtypeStruct((1, 1), f32),
+            jax.ShapeDtypeStruct((1, 1), f32),
+        ),
+        in_specs=[whole] * 5,
+        out_specs=(whole,) * 4,
+        name="factor_update",
+    )(raw_user, raw_item, stats, user, item)
+
+
 def solution(mesh):
     nrow, ncol, nlay = mesh.shape["row"], mesh.shape["col"], mesh.shape["layer"]
 
@@ -419,11 +433,9 @@
         rows, cols = ratings.shape
         rank = user_factor.shape[0] * ncol * nlay
         step = make_step(nrow, ncol, nlay, rank, rows, cols)
-        raw_user, raw_item, stats = step(tile_mask, tile_counts, ratings, user_factor, item_factor)
-        step_size = stats[2, 0]
-        new_user = user_factor - step_size * raw_user
-        new_item = item_factor - step_size * raw_item
-        return (new_user, new_item, stats[0, 0], stats[1, 0])
+        raw_user, raw_item, stats = step(tile_mask.T, tile_counts.T, ratings, user_factor, item_factor)
+        new_user, new_item, loss, norm = update(raw_user, raw_item, stats, user_factor, item_factor)
+        return (new_user, new_item, loss[0, 0], norm[0, 0])
 
     return jax.shard_map(
         body,

time: 46.2 us -> 36 us (0.78)
  other arithmetic: 4.63 us -> 0 us
  local copies, waits for them, and re-layouts: 4.16 us -> 0 us
  Pallas kernels: 36.4 us -> 35.2 us
    sub x2 -> x0, other arithmetic: 4.63 us -> none  [the longest x1 2.37 us: body(): new_user = user_factor - step_size * raw_user]
    unnamed x6 -> x0, local copies, waits for them, and re-layouts: 2.77 us -> none
    slice x1 -> x0, local copies, waits for them, and re-layouts: 1.39 us -> none  [body(): return (new_user, new_item, stats[0, 0], stats[1, 0])]
    pallas_call x1 -> x2, Pallas kernels: 36.4 us -> 35.2 us  [the longest x1 33.2 us: body(): step(tile_mask.T, tile_counts.T, ratings, user_factor, item_factor)]
where the time goes in v2:
time: 36 us; the launch traced here: 35.8 us
  Pallas kernels  35.2 us (98%)
  between operations  0.64 us (2%)
    pallas_call x1, Pallas kernels, body(): step(tile_mask.T, tile_counts.T, ratings, user_factor, item_factor)  33.2 us
    pallas_call x1, Pallas kernels, update(): pl.pallas_call(kernel, out_shape=(jax.ShapeDtypeStruct(user.shape, f32),...  1.94 us

profile of v2, /device:TPU:0, one launch (start us, length us, event | category | flops | bytes accessed | tf_op | source)
XLA Modules:
  0.0 35.8 jit_solution(6309563407918301041)
XLA Ops:
  0.6 33.2 %completion_step.1 = (f32[32,2048]{1,0:T(8,128)}, f32[64,512]{1,0:T(8,128)}, f32[8,128]{1,0:T(8,128)}) custom-call(s32[4,16]{1,0:T(4,128)} %bitcast.4, s32[4,16]{1,0:T(4,128)} %bitcast.5, bf16[2048,512]{1,0:T(8,128)(2,1)} %ratings.1, f32[32,2048]{1,0:T(8,128)} %fu.1, f32[64,512]{1,0:T(8,128)} %fi.1), custom_call_target="tpu_custom_call" | custom-call | tf_op jit(solution)/shard_map/completion_step/pallas_call | solution.py:436
  33.9 1.9 %factor_update.1 = (f32[32,2048]{1,0:T(8,128)}, f32[64,512]{1,0:T(8,128)}, f32[1,1]{1,0:T(1,128)}, f32[1,1]{1,0:T(1,128)}) custom-call(f32[32,2048]{1,0:T(8,128)} %get-tuple-element.11.gu, f32[64,512]{1,0:T(8,128)} %get-tuple-element.12.gi, f32[8,128]{1,0:T(8,128)} %get-tuple-element.13.st, f32[32,2048]{1,0:T(8,128)} %fu.1, f32[64,512]{1,0:T(8,128)} %fi.1), custom_call_target="tpu_custom_call" | custom-call | tf_op jit(solution)/shard_map/factor_update/pallas_call | solution.py:415

commit v3 on v2

v3 whole, which is shorter than its diff:
```python
import math

import jax
import jax.numpy as jnp
from jax import lax
from jax.experimental import pallas as pl
from jax.experimental.pallas import tpu as pltpu
from jax.sharding import PartitionSpec as P

TILE = 128
epsilon = 1e-12
trust_ratio = 0.2
MESH = pl.DeviceIdType.MESH
CHUNKS = 2
AHEAD = 2
LAG = 2


def fold(value):
    flat = value.reshape(-1, value.shape[-1])
    rows = jnp.sum(flat.reshape(flat.shape[0] // 8, 8, flat.shape[1]), axis=0)
    total = rows[:, :TILE]
    for start in range(TILE, rows.shape[1], TILE):
        total = total + rows[:, start : start + TILE]
    return total


def make_step(nrow, ncol, nlay, rank, rows, cols):
    side = math.isqrt(ncol)
    ny = nx = side
    if side * side != ncol:
        ny, nx = 1, ncol
    ndev = nrow * ncol * nlay
    nplane = ncol * nlay
    urows, irows = rank // nplane, rank // nrow
    udt = jnp.bfloat16 if urows % 16 == 0 else jnp.float32
    idt = jnp.bfloat16 if irows % 16 == 0 else jnp.float32
    f32, bf16 = jnp.float32, jnp.bfloat16
    nch = CHUNKS
    width = rows // nch

    dls, dzs = range(1, nlay), range(1, nrow)
    corners = [(dy, dx) for dy in range(ny) for dx in range(nx) if dy + dx > 0]
    per_chunk = 2 * len(corners) + len(dls) * (len(corners) + 2)
    n_sems = nch * per_chunk + 2 * len(dzs)

    def kernel(
        mask, counts, ratings, user, item, raw_user, raw_item, stats,
        rat, uf, itf, U, I, pred, scaled, acc, PU, send0, recv0, S,
        send1, recv1, out_u, out_i,
        send_i, recv_i, mine, G, rat_sem, in_sem, out_sem, ssem, rsem, gsend, grecv,
    ):
        z, c, l = lax.axis_index("row"), lax.axis_index("col"), lax.axis_index("layer")
        y, x = c // nx, c % nx

        def at(z_, y_, x_, l_):
            return (z_, y_ * nx + x_, l_)

        def cp(step):
            return at(z, (y + step[0]) % ny, (x + step[1]) % nx, l)

        def lp(dl):
            return at(z, y, x, (l + dl) % nlay)

        def zp(dz):
            return at((z + dz) % nrow, y, x, l)

        def rank_of(y_, x_, l_):
            return (y_ * nx + x_) * nlay + l_

        load_u = pltpu.make_async_copy(user, uf, in_sem.at[0])
        load_i = pltpu.make_async_copy(item, itf, in_sem.at[1])
        load_u.start()
        load_i.start()
        loads = []
        for j in range(nch):
            part = pl.ds(j * width, width)
            load = pltpu.make_async_copy(ratings.at[part], rat.at[part], rat_sem.at[j])
            load.start()
            loads.append(load)

        barrier = pltpu.get_barrier_semaphore()
        peers = (
            [zp(d) for d in dzs] + [cp(d) for d in corners] + [lp(d) for d in dls]
        )
        for peer in peers:
            pl.semaphore_signal(barrier, inc=1, device_id=peer, device_id_type=MESH)

        me = rank_of(y, x, l)
        load_i.wait()
        I[z] = itf[...].astype(bf16).astype(idt)
        load_u.wait()
        for j in range(nch):
            U[j, me] = uf[:, j * width : (j + 1) * width].astype(bf16).astype(udt)
        pl.semaphore_wait(barrier, len(peers))

        used = [0]
        pending = []

        def send(src, dst, peer):
            n = used[0]
            used[0] += 1
            copy = pltpu.make_async_remote_copy(
                src_ref=src, dst_ref=dst, send_sem=ssem.at[n], recv_sem=rsem.at[n],
                device_id=peer, device_id_type=MESH,
            )
            copy.start()
            pending.append(copy)
            return copy

        gathers_i = [send(I.at[z], I.at[z], zp(d)) for d in dzs]

        got_c, got_l = {}, {}

        def own(j):
            b = U.at[j, me]
            got_c[j] = [send(b, b, cp(d)) for d in corners]
            got_l[j] = [send(b, b, lp(d)) for d in dls]

        def relay(j):
            for (dy, dx), copy in zip(corners, got_c[j]):
                copy.wait_recv()
                b = U.at[j, rank_of((y + ny - dy) % ny, (x + nx - dx) % nx, l)]
                got_l[j] += [send(b, b, lp(d)) for d in dls]

        position = lax.broadcasted_iota(jnp.int32, (TILE, TILE), 0) * TILE + lax.broadcasted_iota(
            jnp.int32, (TILE, TILE), 1
        )
        got_0 = {}
        got_z = []

        def compute(j, error):
            for copy in got_l[j]:
                copy.wait_recv()
            if j == 0:
                for copy in gathers_i:
                    copy.wait_recv()
            loads[j].wait()
            items = I[...].reshape(rank, cols).astype(bf16)
            users = U[j].reshape(rank, width).astype(bf16)
            pred[...] = lax.dot_general(
                users, items, (((0,), (0,)), ((), ())), preferred_element_type=f32
            )

            def tiles(t, total):
                local = pl.ds(pl.multiple_of(t * TILE, TILE), TILE)
                whole = pl.ds(pl.multiple_of(j * width + t * TILE, TILE), TILE)
                row = j * (width // TILE) + t
                for k in range(cols // TILE):
                    lane = slice(k * TILE, (k + 1) * TILE)
                    limit = jnp.where(mask[k, row] == 1, counts[k, row], 0)
                    diff = pred[local, lane] - rat[whole, lane].astype(f32)
                    diff = jnp.where(position < limit, diff, 0.0)
                    scaled[local, lane] = diff.astype(bf16)
                    total = total + fold(diff * diff)
                return total

            error = lax.fori_loop(0, width // TILE, tiles, error)
            sc = scaled[...]
            grad = jnp.dot(users, sc, preferred_element_type=f32).reshape(nrow, irows, cols)
            if j == 0:
                acc[...] = grad
            else:
                acc[...] += grad
            if j == nch - 1:
                for dz in dzs:
                    send_i[dz - 1] = acc[(z + dz) % nrow].astype(idt)
                    got_z.append(send(send_i.at[dz - 1], recv_i.at[dz - 1], zp(dz)))
            PU[j] = lax.dot_general(
                items, sc, (((1,), (1,)), ((), ())), preferred_element_type=f32
            ).reshape(ncol, nlay, urows, width)
            got_0[j] = []
            for dl in dls:
                send0[j, dl - 1] = PU[j, :, (l + dl) % nlay].astype(udt)
                got_0[j].append(send(send0.at[j, dl - 1], recv0.at[j, dl - 1], lp(dl)))
            return error

        got_1 = {}

        def rs1(j):
            total = PU[j, :, l]
            for dl, copy in zip(dls, got_0[j]):
                copy.wait_recv()
                total = total + recv0[j, dl - 1].astype(f32)
            S[j] = total.reshape(ny, nx, urows, width)
            got_1[j] = []
            for n, step in enumerate(corners):
                send1[j, n] = S[j, (y + step[0]) % ny, (x + step[1]) % nx].astype(udt)
                got_1[j].append(send(send1.at[j, n], recv1.at[j, n], cp(step)))

        def rs2(j, grads):
            total = S[j, y, x]
            for n, copy in enumerate(got_1[j]):
                copy.wait_recv()
                total = total + recv1[j, n].astype(f32)
            out_u[:, j * width : (j + 1) * width] = total
            return grads + fold(total * total)

        error = jnp.zeros((8, TILE), f32)
        grads = jnp.zeros((8, TILE), f32)
        for j in range(nch):
            own(j)
        factor = fold(uf[...] * uf[...]) + fold(itf[...] * itf[...])
        for j in range(min(AHEAD, nch)):
            relay(j)
        for j in range(nch):
            error = compute(j, error)
            if j + AHEAD < nch:
                relay(j + AHEAD)
            if j >= LAG:
                rs1(j - LAG)
        for j in range(max(nch - LAG, 0), nch):
            rs1(j)
        for j in range(nch):
            grads = rs2(j, grads)

        total = acc[z]
        for dz, copy in zip(dzs, got_z):
            copy.wait_recv()
            total = total + recv_i[dz - 1].astype(f32)
        out_i[...] = total
        grads = grads + fold(total * total)

        store_u = pltpu.make_async_copy(out_u, raw_user, out_sem.at[0])
        store_i = pltpu.make_async_copy(out_i, raw_item, out_sem.at[1])
        store_u.start()
        store_i.start()

        def count_of(t, total):
            for k in range(cols // TILE):
                total = total + jnp.where(mask[k, t] == 1, counts[k, t], 0)
            return total

        count = lax.fori_loop(0, rows // TILE, count_of, jnp.int32(0)).astype(f32)
        sub = lax.broadcasted_iota(jnp.int32, (8, TILE), 0)
        lane = lax.broadcasted_iota(jnp.int32, (8, TILE), 1)

        def spread(value):
            return jnp.broadcast_to(jnp.sum(value, axis=0, keepdims=True), (8, TILE))

        tile = jnp.where((sub == 3) & (lane == 0), count, 0.0)
        tile = jnp.where(sub == 0, spread(error), tile)
        tile = jnp.where(sub == 1, spread(factor), tile)
        tile = jnp.where(sub == 2, spread(grads), tile)
        mine[...] = tile
        flat = (z * ncol + c) * nlay + l
        G[flat] = tile

        def share(delta):
            to = (flat + delta) % ndev
            return pltpu.make_async_remote_copy(
                src_ref=mine, dst_ref=G.at[flat], send_sem=gsend, recv_sem=grecv,
                device_id=(to // nplane, (to // nlay) % ncol, to % nlay), device_id_type=MESH,
            )

        @pl.loop(1, ndev)
        def _(delta):
            share(delta).start()

        every = pl.ds(0, ndev - 1)
        pltpu.make_async_copy(G.at[every], G.at[every], grecv).wait()
        total = jnp.sum(G[...], axis=0)

        def pick(n):
            return jnp.sum(total[n : n + 1], axis=1, keepdims=True)

        error_sum, factor_sum, grad_sum = pick(0), pick(1), pick(2)
        observed = jnp.maximum(pick(3), 1.0)
        loss = error_sum / observed
        grad_norm = 2.0 / observed * jnp.sqrt(grad_sum + epsilon)
        rate = trust_ratio * jnp.sqrt(factor_sum + epsilon) / grad_norm
        step = rate * (2.0 / observed)
        result = jnp.where(sub == 0, loss, jnp.where(sub == 1, grad_norm, step))
        stats[...] = result
        for copy in pending:
            copy.wait_send()
        pltpu.make_async_copy(G.at[every], G.at[every], gsend).wait()
        store_u.wait()
        store_i.wait()

    vm = pltpu.VMEM
    dma = pltpu.SemaphoreType.DMA
    mc, ml, mz = max(len(corners), 1), max(nlay - 1, 1), max(nrow - 1, 1)
    smem = pl.BlockSpec(memory_space=pltpu.SMEM)
    hbm = pl.BlockSpec(memory_space=pl.ANY)
    return pl.pallas_call(
        kernel,
        out_shape=(
            jax.ShapeDtypeStruct((urows, rows), f32),
            jax.ShapeDtypeStruct((irows, cols), f32),
            jax.ShapeDtypeStruct((8, TILE), f32),
        ),
        in_specs=[smem, smem, hbm, hbm, hbm],
        out_specs=(hbm, hbm, pl.BlockSpec(memory_space=pltpu.VMEM)),
        scratch_shapes=[
            vm((rows, cols), bf16),
            vm((urows, rows), f32),
            vm((irows, cols), f32),
            vm((nch, nplane, urows, width), udt),
            vm((nrow, irows, cols), idt),
            vm((width, cols), f32),
            vm((width, cols), bf16),
            vm((nrow, irows, cols), f32),
            vm((nch, ncol, nlay, urows, width), f32),
            vm((nch, ml, ncol, urows, width), udt),
            vm((nch, ml, ncol, urows, width), udt),
            vm((nch, ny, nx, urows, width), f32),
            vm((nch, mc, urows, width), udt),
            vm((nch, mc, urows, width), udt),
            vm((urows, rows), f32),
            vm((irows, cols), f32),
            vm((mz, irows, cols), idt),
            vm((mz, irows, cols), idt),
            vm((8, TILE), f32),
            vm((ndev, 8, TILE), f32),
            dma((nch,)),
            dma((2,)),
            dma((2,)),
            dma((n_sems,)),
            dma((n_sems,)),
            dma(()),
            dma(()),
        ],
        compiler_params=pltpu.CompilerParams(collective_id=0, has_side_effects=True),
        name="completion_step",
    )


def update(raw_user, raw_item, stats, user, item):
    def kernel(gu, gi, st, fu, fi, new_u, new_i, loss, norm):
        step = st[2:3, 0:1]
        new_i[...] = fi[...] - step * gi[...]
        new_u[...] = fu[...] - step * gu[...]
        loss[...] = st[0:1, 0:1]
        norm[...] = st[1:2, 0:1]

    f32 = jnp.float32
    whole = pl.BlockSpec(memory_space=pltpu.VMEM)
    return pl.pallas_call(
        kernel,
        out_shape=(
            jax.ShapeDtypeStruct(user.shape, f32),
            jax.ShapeDtypeStruct(item.shape, f32),
            jax.ShapeDtypeStruct((1, 1), f32),
            jax.ShapeDtypeStruct((1, 1), f32),
        ),
        in_specs=[whole] * 5,
        out_specs=(whole,) * 4,
        name="factor_update",
    )(raw_user, raw_item, stats, user, item)


def solution(mesh):
    nrow, ncol, nlay = mesh.shape["row"], mesh.shape["col"], mesh.shape["layer"]

    def body(ratings, tile_mask, tile_counts, user_factor, item_factor):
        rows, cols = ratings.shape
        rank = user_factor.shape[0] * ncol * nlay
        step = make_step(nrow, ncol, nlay, rank, rows, cols)
        raw_user, raw_item, stats = step(tile_mask.T, tile_counts.T, ratings, user_factor, item_factor)
        new_user, new_item, loss, norm = update(raw_user, raw_item, stats, user_factor, item_factor)
        return (new_user, new_item, loss[0, 0], norm[0, 0])

    return jax.shard_map(
        body,
        mesh=mesh,
        in_specs=(
            P("row", ("col", "layer")),
            P("row", ("col", "layer")),
            P("row", ("col", "layer")),
            P(("col", "layer"), "row"),
            P("row", ("col", "layer")),
        ),
        out_specs=(P(("col", "layer"), "row"), P("row", ("col", "layer")), P(), P()),
        check_vma=False,
    )
```

time: 36 us -> 34.1 us (0.947)
  Pallas kernels: 35.2 us -> 33.3 us
    pallas_call x1, Pallas kernels: 33.2 us -> 31.4 us  [body(): step(tile_mask.T, tile_counts.T, ratings, user_factor, item_factor)]
where the time goes in v3:
time: 34.1 us; the launch traced here: 33.9 us
  Pallas kernels  33.3 us (98%)
  between operations  0.64 us (2%)
    pallas_call x1, Pallas kernels, body(): step(tile_mask.T, tile_counts.T, ratings, user_factor, item_factor)  31.4 us
    pallas_call x1, Pallas kernels, update(): pl.pallas_call(kernel, out_shape=(jax.ShapeDtypeStruct(user.shape, f32),...  1.94 us

profile of v3, /device:TPU:0, one launch (start us, length us, event | category | flops | bytes accessed | tf_op | source)
XLA Modules:
  0.0 33.9 jit_solution(14523947521881355997)
XLA Ops:
  0.6 31.4 %completion_step.1 = (f32[32,2048]{1,0:T(8,128)}, f32[64,512]{1,0:T(8,128)}, f32[8,128]{1,0:T(8,128)}) custom-call(s32[4,16]{1,0:T(4,128)} %bitcast.4, s32[4,16]{1,0:T(4,128)} %bitcast.5, bf16[2048,512]{1,0:T(8,128)(2,1)} %ratings.1, f32[32,2048]{1,0:T(8,128)} %fu.1, f32[64,512]{1,0:T(8,128)} %fi.1), custom_call_target="tpu_custom_call" | custom-call | tf_op jit(solution)/shard_map/completion_step/pallas_call | solution.py:360
  32.0 1.9 %factor_update.1 = (f32[32,2048]{1,0:T(8,128)}, f32[64,512]{1,0:T(8,128)}, f32[1,1]{1,0:T(1,128)}, f32[1,1]{1,0:T(1,128)}) custom-call(f32[32,2048]{1,0:T(8,128)} %get-tuple-element.11.gu, f32[64,512]{1,0:T(8,128)} %get-tuple-element.12.gi, f32[8,128]{1,0:T(8,128)} %get-tuple-element.13.st, f32[32,2048]{1,0:T(8,128)} %fu.1, f32[64,512]{1,0:T(8,128)} %fi.1), custom_call_target="tpu_custom_call" | custom-call | tf_op jit(solution)/shard_map/factor_update/pallas_call | solution.py:339
